TPU v7x, 1024 devices: a whole 8x8x8 slice. The times are simulated.
1024 devices in a mesh: expert: 32 (over z, x_hi), dp: 32 (over y, x_lo, core).
Axes of the slice: x: 8 (x_hi: 4, x_lo: 2; x = x_hi * 2 + x_lo), y: 8, z: 8, core: 2. Of those that a mesh axis runs over, the one named last changes fastest.
Arguments:
- tokens: bfloat16 [8192, 64, 384], P(('expert', 'dp')), may hold values from -6 to 6
- router: bfloat16 [384, 32], replicated, may hold values from -8.675276 to 8.675276
- w_in: bfloat16 [32, 384, 1536], P('expert'), may hold values from -0.3125 to 0.3125
- w_out: bfloat16 [32, 384, 1536], P('expert'), may hold values from -0.15625 to 0.15625
- out_grad: bfloat16 [8192, 64, 384], P(('expert', 'dp')), may hold values from -6 to 6
Outputs:
- tokens_grad: bfloat16 [8192, 64, 384], P(('expert', 'dp'))
- w_in_grad: float32 [32, 384, 1536], P('expert', 'dp')
- w_out_grad: float32 [32, 384, 1536], P('expert', 'dp')
- router_grad: float32 [384, 32], P('dp')
All inputs are finite; a program needn't handle non-finite values.
Results may differ from a plain program's by a relative error of at most 0.029.
Values may be sent and summed in bfloat16 or wider, within the bound.
A program may use at most 64 MiB of HBM per device.

v0:
```python
import math

import jax
import jax.numpy as jnp
from jax import lax
from jax.sharding import PartitionSpec as P

D = 384


def gelu_pair(value):
    coef = math.sqrt(2.0 / math.pi)
    inner = coef * (value + 0.044715 * value * value * value)
    tangent = jnp.tanh(inner)
    result = 0.5 * value * (1.0 + tangent)
    slope = 0.5 * (1.0 + tangent) + 0.5 * value * (1.0 - tangent * tangent) * coef * (
        1.0 + 3.0 * 0.044715 * value * value
    )
    return (result, slope)


def on_device(tokens, router, w_in, w_out, out_grad):
    f32 = jnp.float32
    bf16 = jnp.bfloat16
    owners = lax.axis_size("expert")
    images = tokens.shape[0]
    experts_all = router.shape[1]
    per_owner = w_in.shape[0]
    row_count = D // lax.axis_size("dp")
    logits = jnp.einsum("bmd,de->bme", tokens, router, preferred_element_type=f32)
    dispatch = jax.nn.softmax(logits, axis=1)
    combine = jax.nn.softmax(logits, axis=2)
    dispatch_b = dispatch.astype(bf16)
    combine_b = combine.astype(bf16)
    slot_in = jnp.einsum("bme,bmd->bed", dispatch_b, tokens, preferred_element_type=f32).astype(
        bf16
    )
    slot_grad = jnp.einsum("bme,bmd->bed", combine_b, out_grad, preferred_element_type=f32).astype(
        bf16
    )
    slot_in = slot_in.reshape(images, owners, per_owner, D)
    slot_grad = slot_grad.reshape(images, owners, per_owner, D)
    recv_in, recv_grad = (
        lax.all_to_all(slot_in, "expert", split_axis=1, concat_axis=1, tiled=True),
        lax.all_to_all(slot_grad, "expert", split_axis=1, concat_axis=1, tiled=True),
    )
    pre_act = jnp.einsum("bskd,kdf->bskf", recv_in, w_in, preferred_element_type=f32)
    value, slope = gelu_pair(pre_act)
    hidden = value.astype(bf16)
    slot_out = jnp.einsum("bskf,kdf->bskd", hidden, w_out, preferred_element_type=f32).astype(bf16)
    hid_grad = jnp.einsum("bskd,kdf->bskf", recv_grad, w_out, preferred_element_type=f32)
    pre_grad = (hid_grad * slope).astype(bf16)
    back_grad = jnp.einsum("bskf,kdf->bskd", pre_grad, w_in, preferred_element_type=f32).astype(
        bf16
    )
    win_term = jnp.einsum("bskd,bskf->dkf", recv_in, pre_grad, preferred_element_type=f32)
    wout_term = jnp.einsum("bskd,bskf->dkf", recv_grad, hidden, preferred_element_type=f32)
    win_part, wout_part = (
        lax.psum_scatter(
            win_term.astype(jnp.bfloat16), "dp", scatter_dimension=0, tiled=True
        ).astype(jnp.float32),
        lax.psum_scatter(
            wout_term.astype(jnp.bfloat16), "dp", scatter_dimension=0, tiled=True
        ).astype(jnp.float32),
    )
    slot_back, slot_in_grad = (
        lax.all_to_all(slot_out, "expert", split_axis=1, concat_axis=1, tiled=True),
        lax.all_to_all(back_grad, "expert", split_axis=1, concat_axis=1, tiled=True),
    )
    slot_back = slot_back.reshape(images, experts_all, D)
    slot_in_grad = slot_in_grad.reshape(images, experts_all, D)
    comb_grad = jnp.einsum("bmd,bed->bme", out_grad, slot_back, preferred_element_type=f32)
    disp_grad = jnp.einsum("bmd,bed->bme", tokens, slot_in_grad, preferred_element_type=f32)
    logit_grad = combine * (comb_grad - jnp.sum(combine * comb_grad, axis=2, keepdims=True))
    logit_grad = logit_grad + dispatch * (
        disp_grad - jnp.sum(dispatch * disp_grad, axis=1, keepdims=True)
    )
    logit_grad = logit_grad.astype(bf16)
    tokens_grad = jnp.einsum("bme,bed->bmd", dispatch_b, slot_in_grad, preferred_element_type=f32)
    tokens_grad = tokens_grad + jnp.einsum(
        "bme,de->bmd", logit_grad, router, preferred_element_type=f32
    )
    tokens_grad = tokens_grad.astype(bf16)
    router_local = jnp.einsum("bmd,bme->de", tokens, logit_grad, preferred_element_type=f32)
    router_full = lax.psum(router_local, ("expert", "dp"))
    router_grad = lax.dynamic_slice_in_dim(
        router_full, lax.axis_index("dp") * row_count, row_count, 0
    )
    w_in_grad = jnp.transpose(win_part, (1, 0, 2))
    w_out_grad = jnp.transpose(wout_part, (1, 0, 2))
    return (tokens_grad, w_in_grad, w_out_grad, router_grad)


def solution(mesh):
    placed = (
        P(("expert", "dp"), None, None),
        P(),
        P("expert", None, None),
        P("expert", None, None),
        P(("expert", "dp"), None, None),
    )
    return jax.shard_map(
        on_device,
        mesh=mesh,
        in_specs=placed,
        out_specs=(
            P(("expert", "dp"), None, None),
            P("expert", "dp", None),
            P("expert", "dp", None),
            P("dp", None),
        ),
        check_vma=False,
    )
```

profile of v0, /device:TPU:1, one launch (start us, length us, event | category | flops | bytes accessed | tf_op | source)
XLA Modules:
  0.0 346.0 jit_solution(13240882062760699846)
XLA Ops:
  7.2 0.0 copy-start
  7.2 0.0 copy-start.2
  7.2 1.4 fusion.73
  8.6 1.3 fusion.77
  9.9 0.0 copy-start.1
  10.0 1.7 fusion.30
  11.7 0.8 copy.14
  12.4 22.5 %all-to-all-start.1 = ((bf16[8,32,1,384]{3,0,2,1:T(8,128)(2,1)}), bf16[8,32,1,384]{3,0,2,1:T(8,128)(2,1)S(1)}, u32[]{:S(2)}, u32[]{:S(2)}) async-start(bf16[8,32,1,384]{3,0,2,1:T(8,128)(2,1)} %copy.14), calls=%async_computation.1 | async-start | bytes 393216 | tf_op jit(solution)/shard_map/all_to_all | solution.py:44
  35.0 0.3 fusion.78
  35.2 0.0 copy-done.2
  35.3 0.2 fusion.29
  35.5 0.7 copy.12
  36.2 10.4 %all-to-all-done.1 = bf16[8,32,1,384]{3,0,2,1:T(8,128)(2,1)S(1)} async-done(((bf16[8,32,1,384]{3,0,2,1:T(8,128)(2,1)}), bf16[8,32,1,384]{3,0,2,1:T(8,128)(2,1)S(1)}, u32[]{:S(2)}, u32[]{:S(2)}) %all-to-all-start.1) | async-done | bytes 196640 | tf_op jit(solution)/shard_map/all_to_all | solution.py:44
  46.6 5.6 %all-to-all-start = ((bf16[8,32,1,384]{3,0,2,1:T(8,128)(2,1)}), bf16[8,32,1,384]{3,0,2,1:T(8,128)(2,1)S(1)}, u32[]{:S(2)}, u32[]{:S(2)}) async-start(bf16[8,32,1,384]{3,0,2,1:T(8,128)(2,1)} %copy.12), calls=%async_computation | async-start | bytes 393216 | tf_op jit(solution)/shard_map/all_to_all | solution.py:45
  52.1 0.0 all-reduce.5.cloned.1.call-start
  52.2 0.0 copy-done.1
  52.2 1.7 convolution_bitcast_fusion.2
  53.9 9.8 %all-to-all-done = bf16[8,32,1,384]{3,0,2,1:T(8,128)(2,1)S(1)} async-done(((bf16[8,32,1,384]{3,0,2,1:T(8,128)(2,1)}), bf16[8,32,1,384]{3,0,2,1:T(8,128)(2,1)S(1)}, u32[]{:S(2)}, u32[]{:S(2)}) %all-to-all-start) | async-done | bytes 196640 | tf_op jit(solution)/shard_map/all_to_all | solution.py:45
  63.7 0.0 copy-done
  63.7 2.6 fusion.10
  66.3 0.0 copy-start.4
  66.3 0.9 copy-done.4
  67.2 1.6 fusion.9
  68.8 6.7 %copy.20 = bf16[384,1,1536]{2,1,0:T(2,128)(2,1)} copy(bf16[384,1,1536]{0,2,1:T(8,128)(2,1)} %fusion.9) | data formatting | bytes 2359296 | tf_op jit(solution)/shard_map/convert_element_type | solution.py:60
  75.5 3.3 fusion.8
  78.8 6.7 %copy.21 = bf16[384,1,1536]{2,1,0:T(2,128)(2,1)} copy(bf16[384,1,1536]{0,2,1:T(8,128)(2,1)} %fusion.8) | data formatting | bytes 2359296 | tf_op jit(solution)/shard_map/convert_element_type | solution.py:63
  85.5 0.0 all-reduce.5.cloned.1.call-update
  85.5 2.0 fusion.36
  87.5 0.8 copy.18
  88.3 5.6 %all-to-all-start.3 = ((bf16[8,32,1,384]{3,0,2,1:T(8,128)(2,1)}), bf16[8,32,1,384]{3,0,2,1:T(8,128)(2,1)S(1)}, u32[]{:S(2)}, u32[]{:S(2)}) async-start(bf16[8,32,1,384]{3,0,2,1:T(8,128)(2,1)} %copy.18), calls=%async_computation.3 | async-start | bytes 393216 | tf_op jit(solution)/shard_map/all_to_all | solution.py:67
  93.9 1.3 dynamic-slice
  95.8 1.7 fusion.33
  97.5 0.0 copy-start.3
  97.5 0.7 copy.16
  98.3 7.2 %all-to-all-done.3 = bf16[8,32,1,384]{3,0,2,1:T(8,128)(2,1)S(1)} async-done(((bf16[8,32,1,384]{3,0,2,1:T(8,128)(2,1)}), bf16[8,32,1,384]{3,0,2,1:T(8,128)(2,1)S(1)}, u32[]{:S(2)}, u32[]{:S(2)}) %all-to-all-start.3) | async-done | bytes 196640 | tf_op jit(solution)/shard_map/all_to_all | solution.py:67
  105.4 5.5 %all-to-all-start.2 = ((bf16[8,32,1,384]{3,0,2,1:T(8,128)(2,1)}), bf16[8,32,1,384]{3,0,2,1:T(8,128)(2,1)S(1)}, u32[]{:S(2)}, u32[]{:S(2)}) async-start(bf16[8,32,1,384]{3,0,2,1:T(8,128)(2,1)} %copy.16), calls=%async_computation.2 | async-start | bytes 393216 | tf_op jit(solution)/shard_map/all_to_all | solution.py:68
  111.0 0.2 convolution_bitcast_fusion.5
  111.2 0.2 fusion.45
  111.5 0.0 copy-start.5
  111.5 12.8 %all-to-all-done.2 = bf16[8,32,1,384]{3,0,2,1:T(8,128)(2,1)S(1)} async-done(((bf16[8,32,1,384]{3,0,2,1:T(8,128)(2,1)}), bf16[8,32,1,384]{3,0,2,1:T(8,128)(2,1)S(1)}, u32[]{:S(2)}, u32[]{:S(2)}) %all-to-all-start.2) | async-done | bytes 196640 | tf_op jit(solution)/shard_map/all_to_all | solution.py:68
  124.3 0.0 copy-done.3
  124.3 0.2 convolution_bitcast_fusion.4
  124.5 1.0 convolution_bitcast_fusion.6
  125.6 115.8 %psum.7 = f32[384,32]{0,1:T(8,128)S(1)} all-reduce(f32[384,32]{0,1:T(8,128)S(1)} %convolution_bitcast_fusion.6), channel_id=1, replica_groups=mesh['expert'=32,'dp'=32] {'expert','dp'}, use_global_device_ids=true, to_apply=%region_8.0 | all-reduce | flops 12288 | bytes 98304 | tf_op jit(solution)/shard_map/psum | solution.py:85
  241.4 0.1 constant_dynamic-slice_fusion
  241.5 0.7 copy.22
  242.1 0.7 fusion.55
  242.8 0.0 copy-done.5
  242.8 1.9 fusion.16
  244.7 92.6 %all-reduce.5.cloned.1.call-done = (bf16[384,1,1536]{2,1,0:T(2,128)(2,1)}, bf16[384,1,1536]{2,1,0:T(2,128)(2,1)}) async-done(((bf16[384,1,1536]{2,1,0:T(2,128)(2,1)}, bf16[384,1,1536]{2,1,0:T(2,128)(2,1)}), (bf16[384,1,1536]{2,1,0:T(2,128)(2,1)}, bf16[384,1,1536]{2,1,0:T(2,128)(2,1)})) %all-reduce.5.cloned.1.call-update) | async-done | bytes 2359312
  337.4 1.7 bitcast_convert_fusion
Async XLA Ops:
  7.2 56.5 %copy-start = (bf16[1,384,1536]{2,1,0:T(8,128)(2,1)S(1)}, bf16[1,384,1536]{2,1,0:T(8,128)(2,1)}, u32[]{:S(2)}) copy-start(bf16[1,384,1536]{2,1,0:T(8,128)(2,1)} %param.8) | copy-start | bytes 3538948
  7.2 28.1 %copy-start.2 = (bf16[8,64,384]{2,1,0:T(8,128)(2,1)S(1)}, bf16[8,64,384]{2,1,0:T(8,128)(2,1)}, u32[]{:S(2)}) copy-start(bf16[8,64,384]{2,1,0:T(8,128)(2,1)} %param.9) | copy-start | bytes 1179652
  9.9 42.2 %copy-start.1 = (bf16[1,384,1536]{2,1,0:T(8,128)(2,1)S(1)}, bf16[1,384,1536]{2,1,0:T(8,128)(2,1)}, u32[]{:S(2)}) copy-start(bf16[1,384,1536]{2,1,0:T(8,128)(2,1)} %param.7) | copy-start | bytes 3538948
  12.4 34.1 %all-to-all-start.1 = ((bf16[8,32,1,384]{3,0,2,1:T(8,128)(2,1)}), bf16[8,32,1,384]{3,0,2,1:T(8,128)(2,1)S(1)}, u32[]{:S(2)}, u32[]{:S(2)}) async-start(bf16[8,32,1,384]{3,0,2,1:T(8,128)(2,1)} %copy.14), calls=%async_computation.1 | async-start | bytes 393216 | tf_op jit(solution)/shard_map/all_to_all | solution.py:44
  46.6 17.2 %all-to-all-start = ((bf16[8,32,1,384]{3,0,2,1:T(8,128)(2,1)}), bf16[8,32,1,384]{3,0,2,1:T(8,128)(2,1)S(1)}, u32[]{:S(2)}, u32[]{:S(2)}) async-start(bf16[8,32,1,384]{3,0,2,1:T(8,128)(2,1)} %copy.12), calls=%async_computation | async-start | bytes 393216 | tf_op jit(solution)/shard_map/all_to_all | solution.py:45
  52.1 285.3 %all-reduce.5.cloned.1.call-start = ((), (), s32[]{:S(2)}) async-start(), calls=%async_computation.4 | async-start | bytes 9437184
  66.3 0.9 copy-start.4
  88.3 17.2 %all-to-all-start.3 = ((bf16[8,32,1,384]{3,0,2,1:T(8,128)(2,1)}), bf16[8,32,1,384]{3,0,2,1:T(8,128)(2,1)S(1)}, u32[]{:S(2)}, u32[]{:S(2)}) async-start(bf16[8,32,1,384]{3,0,2,1:T(8,128)(2,1)} %copy.18), calls=%async_computation.3 | async-start | bytes 393216 | tf_op jit(solution)/shard_map/all_to_all | solution.py:67
  97.5 26.8 %copy-start.3 = (bf16[8,64,384]{2,1,0:T(8,128)(2,1)S(1)}, bf16[8,64,384]{2,1,0:T(8,128)(2,1)}, u32[]{:S(2)}) copy-start(bf16[8,64,384]{2,1,0:T(8,128)(2,1)} %param.5) | copy-start | bytes 1179652
  105.4 18.8 %all-to-all-start.2 = ((bf16[8,32,1,384]{3,0,2,1:T(8,128)(2,1)}), bf16[8,32,1,384]{3,0,2,1:T(8,128)(2,1)S(1)}, u32[]{:S(2)}, u32[]{:S(2)}) async-start(bf16[8,32,1,384]{3,0,2,1:T(8,128)(2,1)} %copy.16), calls=%async_computation.2 | async-start | bytes 393216 | tf_op jit(solution)/shard_map/all_to_all | solution.py:68
  111.5 131.4 %copy-start.5 = (bf16[384,32]{0,1:T(8,128)(2,1)S(1)}, bf16[384,32]{0,1:T(8,128)(2,1)}, u32[]{:S(2)}) copy-start(bf16[384,32]{0,1:T(8,128)(2,1)} %param.6) | copy-start | bytes 73732
Sparse Core Ops, SparseCore 0:
  85.6 251.7 all-reduce.4
where the time goes:
time: 347 us; the launch traced here: 346 us
  waiting for transfers between devices  133 us (38%)
  blocking collectives  116 us (33%)
  starting transfers between devices  39.2 us (11%)
  matrix products  20.4 us (6%)
  local copies, waits for them, and re-layouts  19.3 us (6%)
  between operations  14.9 us (4%)
  other arithmetic  3.53 us (1%)
    psum x1, blocking collectives, on_device(): router_full = lax.psum(router_local, ('expert', 'dp'))  116 us
    unnamed x2, waiting for transfers between devices  92.7 us
    all_to_all x1, starting transfers between devices, on_device(): lax.all_to_all(slot_in, 'expert', split_axis=1, concat_axis=1, tiled=True)  22.5 us
    all_to_all x1, waiting for transfers between devices, on_device(): lax.all_to_all(back_grad, 'expert', split_axis=1, concat_axis=1, tiled=True)  12.8 us
    all_to_all x1, waiting for transfers between devices, on_device(): lax.all_to_all(slot_in, 'expert', split_axis=1, concat_axis=1, tiled=True)  10.4 us
    all_to_all x1, waiting for transfers between devices, on_device(): lax.all_to_all(slot_grad, 'expert', split_axis=1, concat_axis=1, tiled=True)  9.79 us
    all_to_all x1, waiting for transfers between devices, on_device(): lax.all_to_all(slot_out, 'expert', split_axis=1, concat_axis=1, tiled=True)  7.18 us
  transfers between devices with their start and end apart: 5, of which 5 were waited for; matrix products, arithmetic and copies ran while one was open for 4% of the time, Pallas kernels for 0%

commit v1 on v0

v1 whole, which is shorter than its diff:
```python
import functools
import math

import jax
import jax.numpy as jnp
from jax import lax
from jax.experimental import pallas as pl
from jax.experimental.pallas import tpu as pltpu
from jax.sharding import PartitionSpec as P

MESH = pl.DeviceIdType.MESH
F32 = jnp.float32
BF16 = jnp.bfloat16

D = 384
FF = 1536
M = 64
IMG = 8
TOK = IMG * M
NE = 32
NDP = 32
NY = 8
RING = D // NY
ROWS = D // NDP
SLOTS = NE * IMG
CHUNK = 512
NN = (((1,), (0,)), ((), ()))
NT = (((1,), (1,)), ((), ()))
TN = (((0,), (0,)), ((), ()))


def dot(a, b, dims):
    return lax.dot_general(a, b, dims, preferred_element_type=F32)


def iota(shape, axis):
    return lax.broadcasted_iota(jnp.int32, shape, axis)


def mask01(condition):
    return jnp.where(condition, 1.0, 0.0).astype(BF16)


def gelu_pair(value):
    coef = math.sqrt(2.0 / math.pi)
    inner = coef * (value + 0.044715 * value * value * value)
    tangent = jnp.tanh(inner)
    result = 0.5 * value * (1.0 + tangent)
    slope = 0.5 * (1.0 + tangent) + 0.5 * value * (1.0 - tangent * tangent) * coef * (
        1.0 + 3.0 * 0.044715 * value * value
    )
    return (result, slope)


def by_image(reduce, fill, value, low):
    first = reduce(jnp.where(low, value, fill), axis=1, keepdims=True)
    second = reduce(jnp.where(low, fill, value), axis=1, keepdims=True)
    return jnp.where(low, first, second)


def kernel(
    tok_hbm,
    og_hbm,
    router_ref,
    win_hbm,
    wout_hbm,
    tok_out,
    dw_out,
    router_out,
    tok,
    og,
    win,
    wout,
    slots_out,
    slots_in,
    back_out,
    back_in,
    act,
    slope,
    disp,
    comb,
    place,
    tok_perm,
    mine,
    theirs,
    partner,
    ring_out,
    ring_in,
    last_out,
    last_in,
    part_out,
    part_in,
    part_sum,
    full_in,
    load_sem,
    slot_sem,
    back_sem,
    pair_sem,
    ring_sem,
    last_sem,
    part_sem,
    full_sem,
):
    e = lax.axis_index("expert")
    d = lax.axis_index("dp")
    y = lax.div(d, 4)
    core = lax.rem(d, 2)

    loads = [
        pltpu.make_async_copy(src, dst, load_sem.at[i])
        for i, (src, dst) in enumerate(
            ((tok_hbm, tok), (og_hbm, og), (win_hbm, win), (wout_hbm, wout))
        )
    ]
    for load in loads:
        load.start()

    barrier = pltpu.get_barrier_semaphore()

    def greet(k, carry):
        pl.semaphore_signal(
            barrier, inc=1, device_id=(lax.rem(e + k, NE), d), device_id_type=MESH
        )
        pl.semaphore_signal(
            barrier, inc=1, device_id=(e, lax.rem(d + k, NDP)), device_id_type=MESH
        )
        return carry

    lax.fori_loop(1, NE, greet, 0)

    loads[0].wait()
    logits = dot(router_ref[...], tok[...], NT)
    top = jnp.max(logits, axis=0, keepdims=True)
    raised = jnp.exp(logits - top)
    combine = raised / jnp.sum(raised, axis=0, keepdims=True)
    low = iota((NE, 128), 1) < M
    parts = []
    for j in range(TOK // 128):
        x = logits[:, 128 * j : 128 * (j + 1)]
        raised = jnp.exp(x - by_image(jnp.max, -jnp.inf, x, low))
        parts.append(raised / by_image(jnp.sum, 0.0, raised, low))
    dispatch = jnp.concatenate(parts, axis=1)
    disp[...] = dispatch
    comb[...] = combine

    spread = mask01(iota((SLOTS, NE), 0) // IMG == iota((SLOTS, NE), 1))
    own_image = iota((SLOTS, TOK), 0) % IMG == iota((SLOTS, TOK), 1) // M
    placed = jnp.where(own_image, dot(spread, dispatch.astype(BF16), NN), 0.0).astype(BF16)
    place[...] = placed
    slots_out[0] = dot(placed, tok[...], NN).astype(BF16)
    pl.semaphore_wait(barrier, 2 * (NE - 1))

    def exchange(src, dst, sems):
        def send(k, carry):
            to = lax.rem(e + k, NE)
            pltpu.make_async_remote_copy(
                src_ref=src.at[pl.ds(pl.multiple_of(to * IMG, IMG), IMG)],
                dst_ref=dst.at[pl.ds(pl.multiple_of(e * IMG, IMG), IMG)],
                send_sem=sems.at[0],
                recv_sem=sems.at[1],
                device_id=(to, d),
                device_id_type=MESH,
            ).start()
            return carry

        lax.fori_loop(1, NE, send, 0)
        own = pl.ds(pl.multiple_of(e * IMG, IMG), IMG)
        pltpu.make_async_copy(src.at[own], dst.at[own], sems.at[1]).start()

    def arrived(dst, sems):
        pltpu.make_async_copy(dst, dst, sems.at[1]).wait()

    def sent(src, sems):
        some = src.at[pl.ds(0, (NE - 1) * IMG)]
        pltpu.make_async_copy(some, some, sems.at[0]).wait()

    exchange(slots_out.at[0], slots_in.at[0], slot_sem.at[0])
    loads[1].wait()
    placed = jnp.where(own_image, dot(spread, combine.astype(BF16), NN), 0.0).astype(BF16)
    slots_out[1] = dot(placed, og[...], NN).astype(BF16)
    exchange(slots_out.at[1], slots_in.at[1], slot_sem.at[1])

    for q in range(4):
        row = iota((3 * NDP, D), 0)
        pick = mask01(iota((3 * NDP, D), 1) == ROWS * (row % NDP) + 4 * (row // NDP) + q)
        tok_perm[:, TOK * q : TOK * (q + 1)] = dot(pick, tok[...], NT).astype(BF16)

    loads[2].wait()
    loads[3].wait()
    arrived(slots_in.at[0], slot_sem.at[0])
    total = jnp.zeros((SLOTS, D), F32)
    for c in range(0, FF, CHUNK):
        value, rise = gelu_pair(dot(slots_in[0], win[:, c : c + CHUNK], NN))
        act[1, :, c : c + CHUNK] = value.astype(BF16)
        slope[:, c : c + CHUNK] = rise
        total = total + dot(value.astype(BF16), wout[:, c : c + CHUNK], NT)
    back_out[0] = total.astype(BF16)
    exchange(back_out.at[0], back_in.at[0], back_sem.at[0])

    arrived(slots_in.at[1], slot_sem.at[1])
    total = jnp.zeros((SLOTS, D), F32)
    for c in range(0, FF, CHUNK):
        grad = dot(slots_in[1], wout[:, c : c + CHUNK], NN)
        grad = (grad * slope[:, c : c + CHUNK]).astype(BF16)
        act[0, :, c : c + CHUNK] = grad
        total = total + dot(grad, win[:, c : c + CHUNK], NT)
    back_out[1] = total.astype(BF16)
    exchange(back_out.at[1], back_in.at[1], back_sem.at[1])

    def weight_term(kind, dst):
        for c in range(0, FF, CHUNK):
            dst[:, c : c + CHUNK] = dot(
                slots_in[kind], act[kind, :, c : c + CHUNK], TN
            ).astype(BF16)

    weight_term(1 - core, theirs)
    pair = pltpu.make_async_remote_copy(
        src_ref=theirs,
        dst_ref=partner,
        send_sem=pair_sem.at[0],
        recv_sem=pair_sem.at[1],
        device_id=(e, d + 1 - 2 * core),
        device_id_type=MESH,
    )
    pair.start()
    weight_term(core, mine)

    sign = 1 - 2 * core

    def at_ring(step):
        return lax.rem(y + sign * step + 2 * NY, NY)

    def ring_copy(slot, way):
        to = lax.rem(y + sign * way + NY, NY) * 4 + lax.rem(d, 4)
        return pltpu.make_async_remote_copy(
            src_ref=ring_out.at[slot],
            dst_ref=ring_in.at[slot],
            send_sem=ring_sem.at[0, slot],
            recv_sem=ring_sem.at[1, slot],
            device_id=(e, to),
            device_id_type=MESH,
        )

    long = [ring_copy(t, 1) for t in range(4)]
    short = [ring_copy(4 + t, -1) for t in range(3)]

    def own_part(step):
        rows = pl.ds(pl.multiple_of(at_ring(step) * RING, 16), RING)
        return mine[rows, :].astype(F32) + partner[rows, :].astype(F32)

    def ring_step(t):
        value = own_part(4 - t)
        if t:
            long[t - 1].wait_recv()
            value = value + ring_in[t - 1].astype(F32)
        ring_out[t] = value.astype(BF16)
        long[t].start()
        if t < 3:
            value = own_part(t - 3)
            if t:
                short[t - 1].wait_recv()
                value = value + ring_in[3 + t].astype(F32)
            ring_out[4 + t] = value.astype(BF16)
            short[t].start()

    pair.wait_recv()
    ring_step(0)

    move = mask01(
        (iota((SLOTS, SLOTS), 1) // IMG == iota((SLOTS, SLOTS), 0) % NE)
        & (iota((SLOTS, SLOTS), 1) % IMG == iota((SLOTS, SLOTS), 0) // NE)
    )

    def per_slot(rows, values):
        rows = dot(move, rows, NN).astype(BF16)
        out = []
        for j in range(TOK // 128):
            both = dot(
                rows[2 * NE * j : 2 * NE * (j + 1)], values[128 * j : 128 * (j + 1)], NT
            )
            out.append(jnp.where(low, both[:NE], both[NE:]))
        return out

    arrived(back_in.at[0], back_sem.at[0])
    comb_grad = jnp.concatenate(per_slot(back_in[0], og), axis=1)
    combine = comb[...]
    comb_part = combine * (comb_grad - jnp.sum(combine * comb_grad, axis=0, keepdims=True))

    ring_step(1)

    arrived(back_in.at[1], back_sem.at[1])
    parts = []
    for j, grad in enumerate(per_slot(back_in[1], tok)):
        share = disp[:, 128 * j : 128 * (j + 1)]
        parts.append(share * (grad - by_image(jnp.sum, 0.0, share * grad, low)))
    logit_grad = (comb_part + jnp.concatenate(parts, axis=1)).astype(BF16)

    blank = jnp.zeros((NE, TOK), BF16)
    spots = jnp.concatenate(
        [
            jnp.concatenate([logit_grad if i == q else blank for i in range(4)], axis=1)
            for q in range(4)
        ],
        axis=0,
    )
    mixed = dot(tok_perm[...], spots, NT)
    mixed = jnp.concatenate([mixed[NDP * g : NDP * (g + 1)] for g in range(3)], axis=1)
    for r in range(NDP):
        part_out[r] = mixed[r : r + 1]

    def spread_part(k, carry):
        to = lax.rem(d + k, NDP)
        pltpu.make_async_remote_copy(
            src_ref=part_out.at[to],
            dst_ref=part_in.at[d],
            send_sem=part_sem.at[0],
            recv_sem=part_sem.at[1],
            device_id=(e, to),
            device_id_type=MESH,
        ).start()
        return carry

    lax.fori_loop(1, NDP, spread_part, 0)
    pltpu.make_async_copy(part_out.at[d], part_in.at[d], part_sem.at[1]).start()

    tok_out[...] = (
        dot(place[...], back_in[1], TN) + dot(logit_grad, router_ref[...], TN)
    ).astype(BF16)

    ring_step(2)

    pltpu.make_async_copy(part_in, part_in, part_sem.at[1]).wait()
    part_sum[...] = jnp.sum(part_in[...], axis=0)

    def spread_full(k, carry):
        pltpu.make_async_remote_copy(
            src_ref=part_sum,
            dst_ref=full_in.at[e],
            send_sem=full_sem.at[0],
            recv_sem=full_sem.at[1],
            device_id=(lax.rem(e + k, NE), d),
            device_id_type=MESH,
        ).start()
        return carry

    lax.fori_loop(1, NE, spread_full, 0)
    pltpu.make_async_copy(part_sum, full_in.at[e], full_sem.at[1]).start()

    ring_step(3)

    long[3].wait_recv()
    short[2].wait_recv()
    value = own_part(0) + ring_in[3].astype(F32) + ring_in[6].astype(F32)
    for i in range(4):
        last_out[i] = value[ROWS * i : ROWS * (i + 1)].astype(BF16)
    me = lax.rem(d, 4)

    def last_send(k, carry):
        to = lax.rem(me + k, 4)
        pltpu.make_async_remote_copy(
            src_ref=last_out.at[to],
            dst_ref=last_in.at[me],
            send_sem=last_sem.at[0],
            recv_sem=last_sem.at[1],
            device_id=(e, d - me + to),
            device_id_type=MESH,
        ).start()
        return carry

    lax.fori_loop(1, 4, last_send, 0)
    pltpu.make_async_copy(last_out.at[me], last_in.at[me], last_sem.at[1]).start()

    pltpu.make_async_copy(full_in, full_in, full_sem.at[1]).wait()
    router_out[...] = jnp.sum(full_in[...], axis=0)

    pltpu.make_async_copy(last_in, last_in, last_sem.at[1]).wait()
    dw_out[0] = last_in[0].astype(F32) + last_in[2].astype(F32)
    dw_out[1] = last_in[1].astype(F32) + last_in[3].astype(F32)

    for kind in range(2):
        sent(slots_out.at[kind], slot_sem.at[kind])
        sent(back_out.at[kind], back_sem.at[kind])
    pair.wait_send()
    for copy in long + short:
        copy.wait_send()
    some = last_out.at[pl.ds(0, 3)]
    pltpu.make_async_copy(some, some, last_sem.at[0]).wait()
    some = part_out.at[pl.ds(0, NDP - 1)]
    pltpu.make_async_copy(some, some, part_sem.at[0]).wait()
    some = full_in.at[pl.ds(0, NE - 1)]
    pltpu.make_async_copy(some, some, full_sem.at[0]).wait()


def on_device(tokens, router, w_in, w_out, out_grad):
    vmem = pl.BlockSpec(memory_space=pltpu.VMEM)
    hbm = pl.BlockSpec(memory_space=pl.ANY)
    dma = pltpu.SemaphoreType.DMA
    tok_grad, dw, router_grad = pl.pallas_call(
        kernel,
        out_shape=(
            jax.ShapeDtypeStruct((TOK, D), BF16),
            jax.ShapeDtypeStruct((2, ROWS, FF), F32),
            jax.ShapeDtypeStruct((1, D), F32),
        ),
        in_specs=[hbm, hbm, vmem, hbm, hbm],
        out_specs=[vmem, vmem, vmem],
        scratch_shapes=[
            pltpu.VMEM((TOK, D), BF16),
            pltpu.VMEM((TOK, D), BF16),
            pltpu.VMEM((D, FF), BF16),
            pltpu.VMEM((D, FF), BF16),
            pltpu.VMEM((2, SLOTS, D), BF16),
            pltpu.VMEM((2, SLOTS, D), BF16),
            pltpu.VMEM((2, SLOTS, D), BF16),
            pltpu.VMEM((2, SLOTS, D), BF16),
            pltpu.VMEM((2, SLOTS, FF), BF16),
            pltpu.VMEM((SLOTS, FF), F32),
            pltpu.VMEM((NE, TOK), F32),
            pltpu.VMEM((NE, TOK), F32),
            pltpu.VMEM((SLOTS, TOK), BF16),
            pltpu.VMEM((3 * NDP, 4 * TOK), BF16),
            pltpu.VMEM((D, FF), BF16),
            pltpu.VMEM((D, FF), BF16),
            pltpu.VMEM((D, FF), BF16),
            pltpu.VMEM((7, RING, FF), BF16),
            pltpu.VMEM((7, RING, FF), BF16),
            pltpu.VMEM((4, ROWS, FF), BF16),
            pltpu.VMEM((4, ROWS, FF), BF16),
            pltpu.VMEM((NDP, 1, D), F32),
            pltpu.VMEM((NDP, 1, D), F32),
            pltpu.VMEM((1, D), F32),
            pltpu.VMEM((NE, 1, D), F32),
            dma((4,)),
            dma((2, 2)),
            dma((2, 2)),
            dma((2,)),
            dma((2, 7)),
            dma((2,)),
            dma((2,)),
            dma((2,)),
        ],
        compiler_params=pltpu.CompilerParams(
            collective_id=0, has_side_effects=True, vmem_limit_bytes=48 << 20
        ),
    )(
        tokens.reshape(TOK, D),
        out_grad.reshape(TOK, D),
        router.T,
        w_in.reshape(D, FF),
        w_out.reshape(D, FF),
    )
    return (
        tok_grad.reshape(IMG, M, D),
        dw[0:1],
        dw[1:2],
        router_grad.reshape(ROWS, NE),
    )


def solution(mesh):
    placed = (
        P(("expert", "dp"), None, None),
        P(),
        P("expert", None, None),
        P("expert", None, None),
        P(("expert", "dp"), None, None),
    )
    return jax.shard_map(
        on_device,
        mesh=mesh,
        in_specs=placed,
        out_specs=(
            P(("expert", "dp"), None, None),
            P("expert", "dp", None),
            P("expert", "dp", None),
            P("dp", None),
        ),
        check_vma=False,
    )
```

time: 347 us -> 75.3 us (0.22)
  waiting for transfers between devices: 133 us -> 0 us
  blocking collectives: 116 us -> 0 us
  Pallas kernels: 0 us -> 66.1 us
  starting transfers between devices: 39.2 us -> 0 us
  matrix products: 20.4 us -> 0 us
  between operations: 14.9 us -> 0.66 us
  local copies, waits for them, and re-layouts: 19.3 us -> 8.12 us
  other arithmetic: 3.53 us -> 0.02 us
    psum x1 -> x0, blocking collectives: 116 us -> none  [on_device(): router_full = lax.psum(router_local, ('expert', 'dp'))]
    unnamed x2 -> x0, waiting for transfers between devices: 92.7 us -> none
    pallas_call x0 -> x1, Pallas kernels: none -> 66.1 us  [on_device(): pl.pallas_call(kernel, out_shape=(jax.ShapeDtypeStruct((TOK, D), BF16), j...]
    all_to_all x4 -> x0, waiting for transfers between devices: 40.1 us -> none  [the longest x1 12.8 us: on_device(): lax.all_to_all(back_grad, 'expert', split_axis=1, concat_axis=1, tiled=True)]
    all_to_all x4 -> x0, starting transfers between devices: 39.2 us -> none  [the longest x1 22.5 us: on_device(): lax.all_to_all(slot_in, 'expert', split_axis=1, concat_axis=1, tiled=True)]
    dot_general x14 -> x0, matrix products: 20.4 us -> none  [the longest x1 3.3 us: on_device(): jnp.einsum('bskd,bskf->dkf', recv_grad, hidden, preferred_element_type=f32)]
    convert_element_type x4 -> x0, local copies, waits for them, and re-layouts: 14.8 us -> none  [the longest x1 6.68 us: on_device(): wout_term.astype(jnp.bfloat16)]
    unnamed x14 -> x13, local copies, waits for them, and re-layouts: 2.88 us -> 7.42 us
  transfers between devices with their start and end apart: 5 -> 0, of which waited for: 5 -> 0; matrix products, arithmetic and copies ran while one was open for 4% -> 0% of each run, Pallas kernels for 0% -> 0%
where the time goes in v1:
time: 75.3 us; the launch traced here: 74.9 us
  Pallas kernels  66.1 us (88%)
  local copies, waits for them, and re-layouts  8.12 us (11%)
    pallas_call x1, Pallas kernels, on_device(): pl.pallas_call(kernel, out_shape=(jax.ShapeDtypeStruct((TOK, D), BF16), j...  66.1 us
    unnamed x13, local copies, waits for them, and re-layouts  7.42 us

profile of v1, /device:TPU:1, one launch (start us, length us, event | category | flops | bytes accessed | tf_op | source)
XLA Modules:
  0.0 74.9 jit_solution(3360522477092021951)
XLA Ops:
  0.6 0.0 copy-start
  0.6 1.3 %copy-done = bf16[1,384,1536]{2,1,0:T(8,128)(2,1)S(1)} copy-done((bf16[1,384,1536]{2,1,0:T(8,128)(2,1)S(1)}, bf16[1,384,1536]{2,1,0:T(8,128)(2,1)}, u32[]{:S(2)}) %copy-start) | copy-done | bytes 1179672
  1.9 0.0 copy-start.1
  1.9 1.3 %copy-done.1 = bf16[1,384,1536]{2,1,0:T(8,128)(2,1)S(1)} copy-done((bf16[1,384,1536]{2,1,0:T(8,128)(2,1)S(1)}, bf16[1,384,1536]{2,1,0:T(8,128)(2,1)}, u32[]{:S(2)}) %copy-start.1) | copy-done | bytes 1179672
  3.2 0.0 copy-start.2
  3.2 1.0 %copy-done.2 = bf16[8,64,384]{2,1,0:T(8,128)(2,1)S(1)} copy-done((bf16[8,64,384]{2,1,0:T(8,128)(2,1)S(1)}, bf16[8,64,384]{2,1,0:T(8,128)(2,1)}, u32[]{:S(2)}) %copy-start.2) | copy-done | bytes 393240
  4.2 0.0 copy-start.3
  4.2 1.0 %copy-done.3 = bf16[8,64,384]{2,1,0:T(8,128)(2,1)S(1)} copy-done((bf16[8,64,384]{2,1,0:T(8,128)(2,1)S(1)}, bf16[8,64,384]{2,1,0:T(8,128)(2,1)}, u32[]{:S(2)}) %copy-start.3) | copy-done | bytes 393240
  5.2 0.0 copy-start.4
  5.2 0.7 copy-done.4
  5.9 66.1 %shard_map.84 = (bf16[512,384]{1,0:T(8,128)(2,1)S(1)}, f32[2,12,1536]{2,1,0:T(8,128)S(1)}, f32[1,384]{1,0:T(1,128)S(1)}) custom-call(bf16[512,384]{1,0:T(8,128)(2,1)S(1)} %bitcast.8, bf16[512,384]{1,0:T(8,128)(2,1)S(1)} %bitcast.9, bf16[32,384]{1,0:T(8,128)(2,1)S(1)} %bitcast.11, bf16[384,1536]{1,0:T(8,128)(2,1)S(1)} %bitcast.6, bf16[384,1536]{1,0:T(8,128)(2,1)S(1)} %bitcast.7), custom_call_target="tpu_custom_call" | custom-call | tf_op jit(solution)/shard_map/pallas_call | solution.py:398
  72.0 0.7 copy.10
  72.7 0.7 copy.9
  73.5 0.7 reshape.31
  74.1 0.7 copy.12
  (2 shorter events, 0.0 us)
Async XLA Ops:
  0.6 1.3 %copy-start = (bf16[1,384,1536]{2,1,0:T(8,128)(2,1)S(1)}, bf16[1,384,1536]{2,1,0:T(8,128)(2,1)}, u32[]{:S(2)}) copy-start(bf16[1,384,1536]{2,1,0:T(8,128)(2,1)} %param.7) | copy-start | bytes 3538948
  1.9 1.3 %copy-start.1 = (bf16[1,384,1536]{2,1,0:T(8,128)(2,1)S(1)}, bf16[1,384,1536]{2,1,0:T(8,128)(2,1)}, u32[]{:S(2)}) copy-start(bf16[1,384,1536]{2,1,0:T(8,128)(2,1)} %param.8) | copy-start | bytes 3538948
  3.2 1.0 %copy-start.2 = (bf16[8,64,384]{2,1,0:T(8,128)(2,1)S(1)}, bf16[8,64,384]{2,1,0:T(8,128)(2,1)}, u32[]{:S(2)}) copy-start(bf16[8,64,384]{2,1,0:T(8,128)(2,1)} %param.5) | copy-start | bytes 1179652
  4.2 1.0 %copy-start.3 = (bf16[8,64,384]{2,1,0:T(8,128)(2,1)S(1)}, bf16[8,64,384]{2,1,0:T(8,128)(2,1)}, u32[]{:S(2)}) copy-start(bf16[8,64,384]{2,1,0:T(8,128)(2,1)} %param.9) | copy-start | bytes 1179652
  5.2 0.7 copy-start.4
